TPU v7x, 32 devices: a whole 2x2x4 slice. The times are simulated.
32 devices in a mesh: row: 8 (over z, core), rep: 4 (over y, x).
Axes of the slice: x: 2, y: 2, z: 4, core: 2. Of those that a mesh axis runs over, the one named last changes fastest.
Arguments:
- features: bfloat16 [4096, 256], P(('row', 'rep')), may hold values from -6 to 6
- weight: bfloat16 [256, 256], replicated, may hold values from -0.375 to 0.375
- cotangent: bfloat16 [4096, 256], P(('row', 'rep')), may hold values from -6 to 6
- adjacency: bfloat16 [8, 4, 24, 128, 128], P('row', 'rep'), may hold values from -0.15625 to 0.15625
- tile_out: int32 [8, 4, 24], P('row', 'rep'), may hold values from 0 to 3
- tile_in: int32 [8, 4, 24], P('row', 'rep'), may hold values from 0 to 7
- live_count: int32 [8, 4], P('row', 'rep'), may hold values from 6 to 24, as said below
Outputs:
- activated: bfloat16 [4096, 256], P(('row', 'rep'))
- weight_grad: float32 [256, 256], replicated
- feature_grad: float32 [4096, 256], P(('row', 'rep'))
Inputs may be any that keep to these rules, and one draw needn't show every extreme that they name: `live_count`: live tile slots of one device; some device has all 24 slots live in every draw.
All inputs are finite; a program needn't handle non-finite values.
Results may differ from a plain program's by a relative error of at most 0.02.
Values may be sent and summed in bfloat16 or wider, within the bound.
A program may use at most 64 MiB of HBM per device.

v0:
```python
import math
import jax
import jax.numpy as jnp
from jax import lax
from jax.sharding import PartitionSpec as P


def tile_sums(adjacency, first_ids, second_ids, live_mask, table, count, transpose_tile):
    slot_count = adjacency.shape[0]
    block_rows = adjacency.shape[1]
    feat_width = table.shape[2]
    group_size = math.gcd(slot_count, 8)
    turns = slot_count // group_size
    items = (
        adjacency.reshape(turns, group_size, block_rows, block_rows),
        first_ids.reshape(turns, group_size),
        second_ids.reshape(turns, group_size),
        live_mask.reshape(turns, group_size),
    )

    def step_group(running, item):
        tile_group, read_ids, write_ids, live_group = item
        inputs = table[read_ids]
        if transpose_tile:
            products = jnp.einsum(
                "gji,gjf->gif", tile_group, inputs, preferred_element_type=jnp.float32
            )
        else:
            products = jnp.einsum(
                "gij,gjf->gif", tile_group, inputs, preferred_element_type=jnp.float32
            )
        onehot = (write_ids[None, :] == jnp.arange(count)[:, None]).astype(
            jnp.float32
        ) * live_group[None, :]
        running = running + jnp.einsum(
            "bg,gif->bif", onehot, products, precision=lax.Precision.HIGHEST
        )
        return (running, None)

    start = jnp.zeros((count, block_rows, feat_width), jnp.float32)
    running, unused = lax.scan(step_group, start, items)
    return running.reshape(count * block_rows, feat_width)


def add_sources(received):
    return jnp.sum(received.astype(jnp.float32), axis=0)


def body(features, weight, cotangent, adjacency, tile_out, tile_in, live_count):
    block_rows = features.shape[0]
    feat_width = features.shape[1]
    row_count = lax.axis_size("row")
    rep_count = lax.axis_size("rep")
    slot_count = adjacency.shape[2]
    adjacency = adjacency.reshape(slot_count, block_rows, block_rows)
    out_ids = tile_out.reshape(slot_count)
    in_ids = tile_in.reshape(slot_count)
    live_mask = (jnp.arange(slot_count) < live_count.reshape(())).astype(jnp.float32)
    gathered = lax.all_gather(features, "row", axis=0, tiled=True).reshape(
        row_count, block_rows, feat_width
    )
    partial_value = tile_sums(adjacency, in_ids, out_ids, live_mask, gathered, rep_count, False)
    aggregated = lax.psum_scatter(
        partial_value.astype(jnp.bfloat16), "rep", scatter_dimension=0, tiled=True
    )
    pre = jnp.dot(aggregated, weight, preferred_element_type=jnp.float32)
    sig = jax.nn.sigmoid(pre)
    activated = (pre * sig).astype(jnp.bfloat16)
    grad_pre = (cotangent.astype(jnp.float32) * sig * (1.0 + pre * (1.0 - sig))).astype(
        jnp.bfloat16
    )
    weight_part = jnp.dot(aggregated.T, grad_pre, preferred_element_type=jnp.float32)
    grad_rows = jnp.dot(grad_pre, weight.T, preferred_element_type=jnp.float32).astype(jnp.bfloat16)
    group_grads = lax.all_gather(grad_rows, "rep", axis=0, tiled=True)
    weight_grad = lax.psum(weight_part, ("row", "rep"))
    group_grads = group_grads.reshape(rep_count, block_rows, feat_width)
    returned = tile_sums(adjacency, out_ids, in_ids, live_mask, group_grads, row_count, True)
    rounded = returned.astype(jnp.bfloat16).reshape(row_count, block_rows, feat_width)
    feature_grad = add_sources(
        lax.all_to_all(rounded, "row", split_axis=0, concat_axis=0, tiled=True)
    )
    return (activated, weight_grad, feature_grad)


def solution(mesh):
    return jax.shard_map(
        body,
        mesh=mesh,
        in_specs=(
            P(("row", "rep"), None),
            P(),
            P(("row", "rep"), None),
            P("row", "rep", None, None, None),
            P("row", "rep", None),
            P("row", "rep", None),
            P("row", "rep"),
        ),
        out_specs=(P(("row", "rep"), None), P(), P(("row", "rep"), None)),
        check_vma=False,
    )
```

profile of v0, /device:TPU:0, one launch (start us, length us, event | category | flops | bytes accessed | tf_op | source)
XLA Modules:
  0.0 231.4 jit_solution(6620039171133740857)
XLA Ops:
  7.9 0.5 broadcast.99
  8.6 0.7 reduce.6
  9.3 0.7 reduce.7
  10.1 16.7 %all_gather.6 = bf16[1024,256]{1,0:T(8,128)(2,1)S(1)} all-gather(bf16[128,256]{1,0:T(8,128)(2,1)} %param.11), channel_id=1, replica_groups=mesh['row'=8,'rep'=4] {'row'}, dimensions={0}, use_global_device_ids=true | all-gather | bytes 589824 | tf_op jit(solution)/shard_map/all_gather | solution.py:59
  26.8 10.8 %while.22 = (s32[]{:T(128)}, f32[4,128,256]{2,0,1:T(4,128)S(1)}, s32[3,8]{1,0:T(4,128)S(1)}, f32[3,8]{1,0:T(4,128)S(1)}, bf16[3,8,128,128]{3,2,1,0:T(8,128)(2,1)...) while((s32[]{:T(128)}, f32[4,128,256]{2,0,1:T(4,128)S(1)}, ...), condition=%wide.region_1.2_spmd.clone, body=%wide.region_0.1_spmd.clone.sunk | while | flops 79955032 | bytes 4985279 | solution.py:41
  26.8 0.6 gather_fusion
  27.4 1.2 fusion.61
  28.7 1.7 convolution_add_fusion.4
  30.5 0.6 gather_fusion
  31.0 1.2 fusion.61
  32.3 1.7 convolution_add_fusion.4
  34.1 0.6 gather_fusion
  34.7 1.2 fusion.61
  35.9 1.7 convolution_add_fusion.4
  37.6 0.8 copy.25
  39.2 24.8 %reduce-scatter.2.cloned.1.call-done = bf16[128,256]{1,0:T(8,128)(2,1)} async-done(((bf16[512,256]{1,0:T(8,128)(2,1)}), bf16[128,256]{1,0:T(8,128)(2,1)}) %reduce-scatter.2.cloned.1.call-update) | async-done | bytes 65552 | tf_op jit(solution)/shard_map/reduce_scatter | solution.py:63
  64.0 1.7 multiply_convert_fusion
  65.9 9.3 %all_gather.7 = bf16[512,256]{1,0:T(8,128)(2,1)S(1)} all-gather(bf16[128,256]{1,0:T(8,128)(2,1)S(1)} %convolution_convert_fusion), channel_id=1, replica_groups=mesh['row'=8,'rep'=4] {'rep'}, dimensions={0}, use_global_device_ids=true | all-gather | bytes 327680 | tf_op jit(solution)/shard_map/all_gather | solution.py:74
  75.2 7.9 %while.23 = (s32[]{:T(128)}, f32[8,128,256]{2,0,1:T(8,128)S(1)}, s32[3,8]{1,0:T(4,128)S(1)}, f32[3,8]{1,0:T(4,128)S(1)}, bf16[3,8,128,128]{2,3,1,0:T(8,128)(2,1)...) while((s32[]{:T(128)}, f32[8,128,256]{2,0,1:T(8,128)S(1)}, ...), condition=%wide.region_5.6_spmd.clone, body=%wide.region_4.5_spmd.clone.sunk | while | flops 92800152 | bytes 6033855 | solution.py:41
  75.3 0.6 gather_fusion.1
  76.1 1.7 convolution_add_fusion.5
  77.9 0.6 gather_fusion.1
  78.8 1.7 convolution_add_fusion.5
  80.6 0.6 gather_fusion.1
  81.4 1.7 convolution_add_fusion.5
  83.1 1.1 copy.24
  84.2 4.8 %all-to-all-start = ((bf16[8,128,256]{2,1,0:T(8,128)(2,1)}), bf16[8,128,256]{2,1,0:T(8,128)(2,1)S(1)}, u32[]{:S(2)}, u32[]{:S(2)}) async-start(bf16[8,128,256]{2,1,0:T(8,128)(2,1)} %copy.24), calls=%async_computation.1 | async-start | bytes 1048576 | tf_op jit(solution)/shard_map/all_to_all | solution.py:80
  89.0 0.9 fusion.31
  90.0 14.4 %all-to-all-done = bf16[8,128,256]{2,1,0:T(8,128)(2,1)S(1)} async-done(((bf16[8,128,256]{2,1,0:T(8,128)(2,1)}), bf16[8,128,256]{2,1,0:T(8,128)(2,1)S(1)}, u32[]{:S(2)}, u32[]{:S(2)}) %all-to-all-start) | async-done | bytes 524320 | tf_op jit(solution)/shard_map/all_to_all | solution.py:80
  104.3 0.7 convert_reduce_fusion
  105.1 117.8 %all-reduce.2.cloned.1.call-done = f32[256,256]{1,0:T(8,128)} async-done(((f32[256,256]{1,0:T(8,128)}), f32[256,256]{1,0:T(8,128)}) %all-reduce.2.cloned.1.call-update) | async-done | bytes 262160 | tf_op jit(solution)/shard_map/psum | solution.py:75
  222.9 1.7 copy.44
  (50 shorter events, 2.5 us)
Async XLA Ops:
  7.2 56.8 %copy-start = (bf16[256,256]{1,0:T(8,128)(2,1)S(1)}, bf16[256,256]{1,0:T(8,128)(2,1)}, u32[]{:S(2)}) copy-start(bf16[256,256]{1,0:T(8,128)(2,1)} %param.12) | copy-start | bytes 393220
  7.2 56.8 %reduce-scatter.2.cloned.1.call-start = ((), (), s32[]{:S(2)}) async-start(), calls=%async_computation.2 | async-start | bytes 327680 | tf_op jit(solution)/shard_map/reduce_scatter | solution.py:63
  7.9 0.7 copy-start.4
  8.6 0.7 copy-start.5
  37.6 1.2 copy-start.1
  38.8 25.2 %copy-start.3 = (bf16[128,256]{1,0:T(8,128)(2,1)S(1)}, bf16[128,256]{1,0:T(8,128)(2,1)}, u32[]{:S(2)}) copy-start(bf16[128,256]{1,0:T(8,128)(2,1)} %param.13) | copy-start | bytes 196612
  84.2 4.8 %copy-start.2 = (bf16[128,256]{1,0:T(8,128)(2,1)S(1)}, bf16[128,256]{1,0:T(8,128)(2,1)}, u32[]{:S(2)}) copy-start(bf16[128,256]{1,0:T(8,128)(2,1)} %reduce-scatter.2.cloned.1.call-done) | copy-start | bytes 196612
  84.2 20.1 %all-to-all-start = ((bf16[8,128,256]{2,1,0:T(8,128)(2,1)}), bf16[8,128,256]{2,1,0:T(8,128)(2,1)S(1)}, u32[]{:S(2)}, u32[]{:S(2)}) async-start(bf16[8,128,256]{2,1,0:T(8,128)(2,1)} %copy.24), calls=%async_computation.1 | async-start | bytes 1048576 | tf_op jit(solution)/shard_map/all_to_all | solution.py:80
  89.0 133.9 %all-reduce.2.cloned.1.call-start = ((), (), s32[]{:S(2)}) async-start(), calls=%async_computation.3 | async-start | bytes 524288 | tf_op jit(solution)/shard_map/psum | solution.py:75
Sparse Core Ops, SparseCore 0:
  38.5 25.4 reduce-scatter.1
  95.9 126.9 all-reduce.1
where the time goes:
time: 232 us; the launch traced here: 231 us
  waiting for transfers between devices  157 us (68%)
  blocking collectives  26 us (11%)
  matrix products  17.5 us (8%)
  between operations  14.8 us (6%)
  local copies, waits for them, and re-layouts  8.77 us (4%)
  starting transfers between devices  4.83 us (2%)
    psum x1, waiting for transfers between devices, body(): weight_grad = lax.psum(weight_part, ('row', 'rep'))  118 us
    reduce_scatter x1, waiting for transfers between devices, body(): lax.psum_scatter(partial_value.astype(jnp.bfloat16), 'rep', scatter_dimen...  24.8 us
    all_gather x1, blocking collectives, body(): lax.all_gather(features, 'row', axis=0, tiled=True)  16.7 us
    all_to_all x1, waiting for transfers between devices, body(): lax.all_to_all(rounded, 'row', split_axis=0, concat_axis=0, tiled=True)  14.4 us
    dot_general x6, matrix products, step_group(): jnp.einsum('bg,gif->bif', onehot, products, precision=lax.Precision.HIGHEST)  10.2 us
    all_gather x1, blocking collectives, body(): group_grads = lax.all_gather(grad_rows, 'rep', axis=0, tiled=True)  9.29 us
    all_to_all x1, starting transfers between devices, body(): lax.all_to_all(rounded, 'row', split_axis=0, concat_axis=0, tiled=True)  4.75 us
  transfers between devices with their start and end apart: 3, of which 3 were waited for; matrix products, arithmetic and copies ran while one was open for 1% of the time, Pallas kernels for 0%

commit v1 on v0

--- a/solution.py
+++ b/solution.py
@@ -72,7 +72,9 @@
     weight_part = jnp.dot(aggregated.T, grad_pre, preferred_element_type=jnp.float32)
     grad_rows = jnp.dot(grad_pre, weight.T, preferred_element_type=jnp.float32).astype(jnp.bfloat16)
     group_grads = lax.all_gather(grad_rows, "rep", axis=0, tiled=True)
-    weight_grad = lax.psum(weight_part, ("row", "rep"))
+    weight_grad = weight_part
+    for over in ("rep", "row"):
+        weight_grad = lax.psum(weight_grad, over)
     group_grads = group_grads.reshape(rep_count, block_rows, feat_width)
     returned = tile_sums(adjacency, out_ids, in_ids, live_mask, group_grads, row_count, True)
     rounded = returned.astype(jnp.bfloat16).reshape(row_count, block_rows, feat_width)

time: 232 us -> 203 us (0.88)
  waiting for transfers between devices: 157 us -> 129 us
    all_to_all x1, waiting for transfers between devices: 14.4 us -> 0.01 us  [body(): lax.all_to_all(rounded, 'row', split_axis=0, concat_axis=0, tiled=True)]
    psum x1 -> x2, waiting for transfers between devices: 118 us -> 104 us  [body(): weight_grad = lax.psum(weight_grad, over)]
  transfers between devices with their start and end apart: 3 -> 4, of which waited for: 3 -> 3; matrix products, arithmetic and copies ran while one was open for 1% -> 1% of each run, Pallas kernels for 0% -> 0%
where the time goes in v1:
time: 203 us
  waiting for transfers between devices  129 us (64%)
  blocking collectives  26 us (13%)
  matrix products  17.5 us (9%)
  between operations  14.5 us (7%)
  local copies, waits for them, and re-layouts  8.77 us (4%)
  starting transfers between devices  4.87 us (2%)
  other arithmetic  2.17 us (1%)
    psum x2, waiting for transfers between devices, body(): weight_grad = lax.psum(weight_grad, over)  104 us
    reduce_scatter x1, waiting for transfers between devices, body(): lax.psum_scatter(partial_value.astype(jnp.bfloat16), 'rep', scatter_dimen...  24.8 us
    all_gather x1, blocking collectives, body(): lax.all_gather(features, 'row', axis=0, tiled=True)  16.7 us
    dot_general x6, matrix products, step_group(): jnp.einsum('bg,gif->bif', onehot, products, precision=lax.Precision.HIGHEST)  10.2 us
    all_gather x1, blocking collectives, body(): group_grads = lax.all_gather(grad_rows, 'rep', axis=0, tiled=True)  9.29 us
    all_to_all x1, starting transfers between devices, body(): lax.all_to_all(rounded, 'row', split_axis=0, concat_axis=0, tiled=True)  4.75 us
  transfers between devices with their start and end apart: 4, of which 3 were waited for; matrix products, arithmetic and copies ran while one was open for 1% of the time, Pallas kernels for 0%

profile of v1, /device:TPU:0, one launch (start us, length us, event | category | flops | bytes accessed | tf_op | source)
XLA Modules:
  0.0 202.8 jit_solution(15856842576006587616)
XLA Ops:
  7.9 0.5 broadcast.99
  8.6 0.7 reduce.6
  9.3 0.7 reduce.7
  10.1 16.7 %all_gather.6 = bf16[1024,256]{1,0:T(8,128)(2,1)S(1)} all-gather(bf16[128,256]{1,0:T(8,128)(2,1)} %param.11), channel_id=1, replica_groups=mesh['row'=8,'rep'=4] {'row'}, dimensions={0}, use_global_device_ids=true | all-gather | bytes 589824 | tf_op jit(solution)/shard_map/all_gather | solution.py:59
  26.8 10.8 %while.22 = (s32[]{:T(128)}, f32[4,128,256]{2,0,1:T(4,128)S(1)}, s32[3,8]{1,0:T(4,128)S(1)}, f32[3,8]{1,0:T(4,128)S(1)}, bf16[3,8,128,128]{3,2,1,0:T(8,128)(2,1)...) while((s32[]{:T(128)}, f32[4,128,256]{2,0,1:T(4,128)S(1)}, ...), condition=%wide.region_1.2_spmd.clone, body=%wide.region_0.1_spmd.clone.sunk | while | flops 79955032 | bytes 4985279 | solution.py:41
  26.8 0.6 gather_fusion
  27.4 1.2 fusion.61
  28.7 1.7 convolution_add_fusion.4
  30.5 0.6 gather_fusion
  31.0 1.2 fusion.61
  32.3 1.7 convolution_add_fusion.4
  34.1 0.6 gather_fusion
  34.7 1.2 fusion.61
  35.9 1.7 convolution_add_fusion.4
  37.6 0.8 copy.25
  39.2 24.8 %reduce-scatter.2.cloned.1.call-done = bf16[128,256]{1,0:T(8,128)(2,1)} async-done(((bf16[512,256]{1,0:T(8,128)(2,1)}), bf16[128,256]{1,0:T(8,128)(2,1)}) %reduce-scatter.2.cloned.1.call-update) | async-done | bytes 65552 | tf_op jit(solution)/shard_map/reduce_scatter | solution.py:63
  64.0 1.7 multiply_convert_fusion
  65.9 9.3 %all_gather.7 = bf16[512,256]{1,0:T(8,128)(2,1)S(1)} all-gather(bf16[128,256]{1,0:T(8,128)(2,1)S(1)} %convolution_convert_fusion), channel_id=1, replica_groups=mesh['row'=8,'rep'=4] {'rep'}, dimensions={0}, use_global_device_ids=true | all-gather | bytes 327680 | tf_op jit(solution)/shard_map/all_gather | solution.py:74
  75.2 7.9 %while.23 = (s32[]{:T(128)}, f32[8,128,256]{2,0,1:T(8,128)S(1)}, s32[3,8]{1,0:T(4,128)S(1)}, f32[3,8]{1,0:T(4,128)S(1)}, bf16[3,8,128,128]{2,3,1,0:T(8,128)(2,1)...) while((s32[]{:T(128)}, f32[8,128,256]{2,0,1:T(8,128)S(1)}, ...), condition=%wide.region_6.7_spmd.clone, body=%wide.region_5.6_spmd.clone.sunk | while | flops 92800152 | bytes 6033855 | solution.py:41
  75.3 0.6 gather_fusion.1
  76.1 1.7 convolution_add_fusion.5
  77.9 0.6 gather_fusion.1
  78.8 1.7 convolution_add_fusion.5
  80.6 0.6 gather_fusion.1
  81.4 1.7 convolution_add_fusion.5
  83.1 1.1 copy.24
  84.2 4.8 %all-to-all-start = ((bf16[8,128,256]{2,1,0:T(8,128)(2,1)}), bf16[8,128,256]{2,1,0:T(8,128)(2,1)S(1)}, u32[]{:S(2)}, u32[]{:S(2)}) async-start(bf16[8,128,256]{2,1,0:T(8,128)(2,1)} %copy.24), calls=%async_computation.1 | async-start | bytes 1048576 | tf_op jit(solution)/shard_map/all_to_all | solution.py:82
  89.0 0.9 fusion.31
  90.0 46.8 %all-reduce.3.cloned.1.call-done = f32[256,256]{1,0:T(8,128)} async-done(((f32[256,256]{1,0:T(8,128)}), f32[256,256]{1,0:T(8,128)}) %all-reduce.3.cloned.1.call-update) | async-done | bytes 262160 | tf_op jit(solution)/shard_map/psum | solution.py:77
  136.9 0.7 convert_reduce_fusion
  137.6 57.0 %all-reduce.5.cloned.1.call-done = f32[256,256]{1,0:T(8,128)} async-done(((f32[256,256]{1,0:T(8,128)}), f32[256,256]{1,0:T(8,128)}) %all-reduce.5.cloned.1.call-update) | async-done | bytes 262160 | tf_op jit(solution)/shard_map/psum | solution.py:77
  194.6 1.7 copy.45
  (53 shorter events, 2.5 us)
Async XLA Ops:
  7.2 56.8 %copy-start = (bf16[256,256]{1,0:T(8,128)(2,1)S(1)}, bf16[256,256]{1,0:T(8,128)(2,1)}, u32[]{:S(2)}) copy-start(bf16[256,256]{1,0:T(8,128)(2,1)} %param.12) | copy-start | bytes 393220
  7.2 56.8 %reduce-scatter.2.cloned.1.call-start = ((), (), s32[]{:S(2)}) async-start(), calls=%async_computation.2 | async-start | bytes 327680 | tf_op jit(solution)/shard_map/reduce_scatter | solution.py:63
  7.9 0.7 copy-start.4
  8.6 0.7 copy-start.5
  37.6 1.2 copy-start.1
  38.8 25.2 %copy-start.3 = (bf16[128,256]{1,0:T(8,128)(2,1)S(1)}, bf16[128,256]{1,0:T(8,128)(2,1)}, u32[]{:S(2)}) copy-start(bf16[128,256]{1,0:T(8,128)(2,1)} %param.13) | copy-start | bytes 196612
  84.2 4.8 %copy-start.2 = (bf16[128,256]{1,0:T(8,128)(2,1)S(1)}, bf16[128,256]{1,0:T(8,128)(2,1)}, u32[]{:S(2)}) copy-start(bf16[128,256]{1,0:T(8,128)(2,1)} %reduce-scatter.2.cloned.1.call-done) | copy-start | bytes 196612
  84.2 52.6 %all-to-all-start = ((bf16[8,128,256]{2,1,0:T(8,128)(2,1)}), bf16[8,128,256]{2,1,0:T(8,128)(2,1)S(1)}, u32[]{:S(2)}, u32[]{:S(2)}) async-start(bf16[8,128,256]{2,1,0:T(8,128)(2,1)} %copy.24), calls=%async_computation.1 | async-start | bytes 1048576 | tf_op jit(solution)/shard_map/all_to_all | solution.py:82
  89.0 47.9 %all-reduce.3.cloned.1.call-start = ((), (), s32[]{:S(2)}) async-start(), calls=%async_computation.3 | async-start | bytes 524288 | tf_op jit(solution)/shard_map/psum | solution.py:77
  90.0 104.6 %all-reduce.5.cloned.1.call-start = ((), (), s32[]{:S(2)}) async-start(), calls=%async_computation.4 | async-start | bytes 524288 | tf_op jit(solution)/shard_map/psum | solution.py:77
Sparse Core Ops, SparseCore 0:
  38.5 25.4 reduce-scatter.1
  93.3 43.5 all-reduce.2
  139.2 55.4 all-reduce.4
